TPU v7x, 32 devices: a whole 2x2x4 slice. The times are simulated.
32 devices in a mesh: seq: 8 (over y, x, core), head: 4 (over z).
Axes of the slice: x: 2, y: 2, z: 4, core: 2. Of those that a mesh axis runs over, the one named last changes fastest.
Arguments:
- queries: bfloat16 [4096, 4096], P('seq', 'head'), may hold values from -8 to 8
- keys: bfloat16 [4096, 4096], P('seq', 'head'), may hold values from -8 to 8
- values: bfloat16 [4096, 4096], P('seq', 'head'), may hold values from -6 to 6
- grad_normed: bfloat16 [4096, 4096], P('seq', 'head'), may hold values from -6 to 6
- docs: int32 [4096], P('seq'), may hold values from 0 to 3, as said below
Outputs:
- normed: bfloat16 [4096, 4096], P('seq', 'head')
- grad_queries: bfloat16 [4096, 4096], P('seq', 'head')
- grad_keys: bfloat16 [4096, 4096], P('seq', 'head')
- grad_values: bfloat16 [4096, 4096], P('seq', 'head')
Inputs may be any that keep to these rules, and one draw needn't show every extreme that they name: docs never falls along the sequence; each of the 4 documents is a run of 1 to 3072 tokens, one of exactly 3072.
All inputs are finite; a program needn't handle non-finite values.
Results may differ from a plain program's by a relative error of at most 0.01.
Values may be sent and summed in bfloat16 or wider, within the bound.
No kernel may reach another device: no remote copies, remote signals or barrier semaphores. Data moves between devices by JAX's collectives and lax.ppermute only.
A program may use at most 192 MiB of HBM per device.

v0:
```python
import functools
import math

import jax
import jax.numpy as jnp
from jax import lax
from jax.experimental import pallas as pl
from jax.experimental.pallas import tpu as pltpu
from jax.sharding import PartitionSpec as P

HEADS = 32
HEAD_DIM = 128


norm_eps = 1e-06

OFFSETS = (0, 1, 2, 4)
NEG = -1e30
F32 = jnp.float32
BF16 = jnp.bfloat16
VMEM_BYTES = 60 * 1024 * 1024


def copy_in(rank, refs, held, sems):
    copies = [
        pltpu.make_async_copy(ref, held.at[rank ^ m], sems.at[m]) for m, ref in enumerate(refs)
    ]
    for copy in copies:
        copy.start()
    for copy in copies:
        copy.wait()


def find_bounds(held, block, bounds):
    ids = held[:, 3 * block :, :].astype(F32)
    for d in range(3):
        count = jnp.sum(jnp.where(ids < d + 0.5, 1.0, 0.0))
        bounds[d] = count.astype(jnp.int32)


def doc_of(position, bounds):
    doc = jnp.int32(0)
    for d in range(3):
        doc = doc + (position >= bounds[d]).astype(jnp.int32)
    return doc


def pair_state(i, off, block, bounds):
    j = jnp.maximum(i - off, 0)
    if off == 0:
        return j, None, None
    active = (i >= off) & (doc_of(i * block, bounds) == doc_of(j * block + block - 1, bounds))
    full = doc_of(j * block, bounds) == doc_of(i * block + block - 1, bounds)
    return j, active, full


def doc_starts(i, block, bounds):
    pos = i * block + lax.broadcasted_iota(jnp.int32, (1, block), 1)
    start = jnp.zeros((1, block), jnp.int32)
    for d in range(3):
        start = jnp.where(pos >= bounds[d], jnp.maximum(start, bounds[d]), start)
    return pos, start


def nt_dot(a, b):
    return lax.dot_general(a, b, (((1,), (1,)), ((), ())), preferred_element_type=F32)


def nn_dot(a, b):
    return lax.dot_general(a, b, (((1,), (0,)), ((), ())), preferred_element_type=F32)


def forward_kernel(block, rank_ref, *refs):
    n = 8
    a_refs = refs[:n]
    prob_ref, out_t_ref, out_ref, inv_ref, square_ref = refs[n : n + 5]
    held, val_t, score, top, total, acc, bounds, sems = refs[n + 5 :]
    i = pl.program_id(0)

    @pl.when(i == 0)
    def _():
        copy_in(rank_ref[0], a_refs, held, sems)
        find_bounds(held, block, bounds)
        for t in range(n):
            val_t[t] = held[t, 2 * block : 3 * block, :].T

    gain = math.log2(math.e) / math.sqrt(HEAD_DIM)
    query = held[i, 0:block, :]
    q_pos, q_start = doc_starts(i, block, bounds)
    pairs = [(off,) + pair_state(i, off, block, bounds) for off in OFFSETS]

    def put_score(slot, off, j, masked):
        s = nt_dot(held[j, block : 2 * block, :], query) * gain
        if masked:
            k_pos = j * block + lax.broadcasted_iota(jnp.int32, (block, 1), 0)
            keep = k_pos >= q_start
            if off == 0:
                keep = keep & (k_pos <= q_pos)
            s = jnp.where(keep, s, NEG)
        score[slot] = s
        peak = jnp.max(s, axis=0, keepdims=True)
        top[...] = peak if off == 0 else jnp.maximum(top[...], peak)

    for slot, (off, j, active, full) in enumerate(pairs):
        if off == 0:
            put_score(slot, off, j, True)
        else:
            pl.when(active & full)(functools.partial(put_score, slot, off, j, False))
            pl.when(active & jnp.logical_not(full))(functools.partial(put_score, slot, off, j, True))

    def take_probs(slot, off, j):
        p = jnp.exp2(score[slot] - top[...])
        row = jnp.sum(p, axis=0, keepdims=True)
        pb = p.astype(BF16)
        prob_ref[0, slot] = pb
        term = nn_dot(val_t[j], pb)
        if off == 0:
            total[...] = row
            acc[...] = term
        else:
            total[...] += row
            acc[...] += term

    for slot, (off, j, active, full) in enumerate(pairs):
        if off == 0:
            take_probs(slot, off, j)
        else:
            pl.when(active)(functools.partial(take_probs, slot, off, j))

    inv = 1.0 / total[...]
    out_t = acc[...] * inv
    out_t_ref[0] = out_t
    out_ref[0] = out_t.T.astype(BF16)
    inv_ref[0] = inv
    square_ref[0] = jnp.sum(out_t * out_t, axis=0, keepdims=True)


def project_kernel(block, rank_ref, *refs):
    n = 8
    g_refs = refs[:n]
    out_t_ref, square_ref, stats_ref, held, sems = refs[n:]
    copy_in(rank_ref[0], g_refs, held, sems)
    for t in range(n):
        cot_t = held[t].astype(F32).T
        cols = slice(t * block, (t + 1) * block)
        stats_ref[0:1, cols] = square_ref[t]
        stats_ref[1:2, cols] = jnp.sum(cot_t * out_t_ref[t], axis=0, keepdims=True)


def backward_kernel(block, rank_ref, *refs):
    n = 8
    a_refs, g_refs = refs[:n], refs[n : 2 * n]
    prob_ref, out_t_ref, inv_ref, stats_ref = refs[2 * n : 2 * n + 4]
    d_refs = refs[2 * n + 4 : 3 * n + 4]
    held, cot, key_t, grad_q, grad_k, grad_v, acc, bounds, sems, sems_g = refs[3 * n + 4 :]
    i = pl.program_id(0)
    scale = 1.0 / math.sqrt(HEAD_DIM)
    width = HEADS * HEAD_DIM

    @pl.when(i == 0)
    def _():
        copies = [
            pltpu.make_async_copy(ref, cot.at[rank_ref[0] ^ m], sems_g.at[m])
            for m, ref in enumerate(g_refs)
        ]
        for copy in copies:
            copy.start()
        copy_in(rank_ref[0], a_refs, held, sems)
        for copy in copies:
            copy.wait()
        find_bounds(held, block, bounds)
        for t in range(n):
            key_t[t] = held[t, block : 2 * block, :].T
        grad_k[...] = jnp.zeros_like(grad_k)
        grad_v[...] = jnp.zeros_like(grad_v)

    inv_rms = lax.rsqrt(stats_ref[0, 0:1, :] / width + norm_eps)
    coef = inv_rms * inv_rms * inv_rms * stats_ref[0, 1:2, :] / width
    out_t = out_t_ref[0]
    dattn_t = (inv_rms * cot[i].astype(F32).T - out_t * coef) * inv_ref[0]
    dattn_tb = dattn_t.astype(BF16)
    dattn_f = dattn_tb.astype(F32)
    delta = jnp.sum(dattn_f * out_t, axis=0, keepdims=True)
    dattn = dattn_f.T.astype(BF16)
    query = held[i, 0:block, :]

    def one_pair(slot, off, j):
        pb = prob_ref[0, slot]
        dprob = nn_dot(held[j, 2 * block : 3 * block, :], dattn_tb)
        ds = (pb.astype(F32) * (dprob - delta)).astype(BF16)
        term = nn_dot(key_t[j], ds)
        if off == 0:
            acc[...] = term
        else:
            acc[...] += term
        grad_k[j] += nn_dot(ds, query)
        grad_v[j] += nn_dot(pb, dattn)

    for slot, off in enumerate(OFFSETS):
        j, active, full = pair_state(i, off, block, bounds)
        if off == 0:
            one_pair(slot, off, j)
        else:
            pl.when(active)(functools.partial(one_pair, slot, off, j))

    grad_q[i] = (acc[...] * scale).T.astype(BF16)

    @pl.when(i == n - 1)
    def _():
        for m in range(n):
            t = rank_ref[0] ^ m
            d_refs[m][0:block, :] = grad_q[t]
            d_refs[m][block : 2 * block, :] = (grad_k[t] * scale).astype(BF16)
            d_refs[m][2 * block :, :] = grad_v[t].astype(BF16)


def pack_kernel(block, rank_ref, q_ref, k_ref, v_ref, g_ref, doc_ref, *refs):
    n = 8
    a_refs, g_refs, sems = refs[:n], refs[n : 2 * n], refs[2 * n]
    copies = []
    for m in range(n):
        cols = pl.ds(pl.multiple_of((rank_ref[0] ^ m) * HEAD_DIM, HEAD_DIM), HEAD_DIM)
        parts = [
            (q_ref.at[:, cols], a_refs[m].at[0:block, :]),
            (k_ref.at[:, cols], a_refs[m].at[block : 2 * block, :]),
            (v_ref.at[:, cols], a_refs[m].at[2 * block : 3 * block, :]),
            (doc_ref, a_refs[m].at[3 * block :, :]),
            (g_ref.at[:, cols], g_refs[m]),
        ]
        for source, target in parts:
            copies.append(pltpu.make_async_copy(source, target, sems.at[len(copies)]))
    for copy in copies:
        copy.start()
    for copy in copies:
        copy.wait()


def unpack_kernel(block, rank_ref, *refs):
    n = 8
    d_refs, outs, sems = refs[:n], refs[n : n + 3], refs[n + 3]
    copies = []
    for m in range(n):
        cols = pl.ds(pl.multiple_of((rank_ref[0] ^ m) * HEAD_DIM, HEAD_DIM), HEAD_DIM)
        for part, out in enumerate(outs):
            rows = slice(part * block, (part + 1) * block)
            copies.append(
                pltpu.make_async_copy(d_refs[m].at[rows, :], out.at[:, cols], sems.at[len(copies)])
            )
    for copy in copies:
        copy.start()
    for copy in copies:
        copy.wait()


def normed_kernel(block, rank_ref, stats_ref, *refs):
    n = 8
    o_refs, out_ref = refs[:n], refs[n]
    inv_rms = lax.rsqrt(stats_ref[0, 0:1, :] / (HEADS * HEAD_DIM) + norm_eps)
    spread = jnp.broadcast_to(inv_rms, (HEAD_DIM, block)).T
    for m in range(n):
        cols = pl.ds(pl.multiple_of((rank_ref[0] ^ m) * HEAD_DIM, HEAD_DIM), HEAD_DIM)
        out_ref[:, cols] = (o_refs[m][...].astype(F32) * spread).astype(BF16)


SMEM_SPEC = pl.BlockSpec(memory_space=pltpu.SMEM)
ANY_SPEC = pl.BlockSpec(memory_space=pl.ANY)
VMEM_SPEC = pl.BlockSpec(memory_space=pltpu.VMEM)


def shape_of(shape, dtype):
    return jax.ShapeDtypeStruct(shape, dtype)


def swap(value, m):
    if m == 0:
        return value
    n = lax.axis_size("seq")
    return lax.ppermute(value, "seq", [(s, s ^ m) for s in range(n)])


def sum_everywhere(stats):
    stats = stats + swap(stats, 1)
    stats = stats + swap(stats, 2) + swap(stats, 4) + swap(stats, 6)
    heads = lax.axis_size("head")
    parts = [
        lax.ppermute(stats, "head", [(s, (s + d) % heads) for s in range(heads)])
        for d in range(1, heads)
    ]
    return functools.reduce(jnp.add, parts, stats)


def by_head(queries, keys, values, grad_normed, docs):
    block, width_dev = queries.shape
    n = width_dev // HEAD_DIM
    rank = lax.axis_index("seq").reshape(1).astype(jnp.int32)
    doc_rows = jnp.pad(
        docs.astype(BF16).reshape(block // 128, 128), ((0, 16 - block // 128), (0, 0)),
        constant_values=4.0,
    )
    rows = 3 * block + 16
    params = pltpu.CompilerParams(vmem_limit_bytes=VMEM_BYTES)
    packed = pl.pallas_call(
        functools.partial(pack_kernel, block),
        out_shape=[shape_of((rows, HEAD_DIM), BF16)] * n + [shape_of((block, HEAD_DIM), BF16)] * n,
        in_specs=[SMEM_SPEC] + [ANY_SPEC] * 5,
        out_specs=[ANY_SPEC] * (2 * n),
        scratch_shapes=[pltpu.SemaphoreType.DMA((5 * n,))],
        name="pack",
    )(rank, queries, keys, values, grad_normed, doc_rows)
    a = [swap(packed[m], m) for m in range(n)]
    g = [swap(packed[n + m], m) for m in range(n)]

    step = lambda *shape: pl.BlockSpec((1,) + shape, lambda i: (i,) + (0,) * len(shape))
    probs, out_t, out, inv_total, square = pl.pallas_call(
        functools.partial(forward_kernel, block),
        grid=(n,),
        out_shape=[
            shape_of((n, len(OFFSETS), block, block), BF16),
            shape_of((n, HEAD_DIM, block), F32),
            shape_of((n, block, HEAD_DIM), BF16),
            shape_of((n, 1, block), F32),
            shape_of((n, 1, block), F32),
        ],
        in_specs=[SMEM_SPEC] + [ANY_SPEC] * n,
        out_specs=[
            step(len(OFFSETS), block, block),
            step(HEAD_DIM, block),
            step(block, HEAD_DIM),
            step(1, block),
            step(1, block),
        ],
        scratch_shapes=[
            pltpu.VMEM((n, rows, HEAD_DIM), BF16),
            pltpu.VMEM((n, HEAD_DIM, block), BF16),
            pltpu.VMEM((len(OFFSETS), block, block), F32),
            pltpu.VMEM((1, block), F32),
            pltpu.VMEM((1, block), F32),
            pltpu.VMEM((HEAD_DIM, block), F32),
            pltpu.SMEM((3,), jnp.int32),
            pltpu.SemaphoreType.DMA((n,)),
        ],
        compiler_params=params,
        name="forward",
    )(rank, *a)

    stats = pl.pallas_call(
        functools.partial(project_kernel, block),
        out_shape=shape_of((2, n * block), F32),
        in_specs=[SMEM_SPEC] + [ANY_SPEC] * n + [VMEM_SPEC] * 2,
        out_specs=VMEM_SPEC,
        scratch_shapes=[
            pltpu.VMEM((n, block, HEAD_DIM), BF16),
            pltpu.SemaphoreType.DMA((n,)),
        ],
        compiler_params=params,
        name="project",
    )(rank, *g, out_t, square)
    stats = sum_everywhere(stats)

    home = [
        swap(lax.dynamic_index_in_dim(out, rank[0] ^ m, 0, keepdims=False), m) for m in range(n)
    ]
    stats_by_block = stats.reshape(2, n, block).transpose(1, 0, 2)
    own_stats = lax.dynamic_slice_in_dim(stats_by_block, rank[0], 1, axis=0)
    normed = pl.pallas_call(
        functools.partial(normed_kernel, block),
        out_shape=shape_of((block, width_dev), BF16),
        in_specs=[SMEM_SPEC] + [VMEM_SPEC] * (n + 1),
        out_specs=VMEM_SPEC,
        compiler_params=params,
        name="normed",
    )(rank, own_stats, *home)

    grads = pl.pallas_call(
        functools.partial(backward_kernel, block),
        grid=(n,),
        out_shape=[shape_of((3 * block, HEAD_DIM), BF16)] * n,
        in_specs=[SMEM_SPEC] + [ANY_SPEC] * (2 * n) + [
            step(len(OFFSETS), block, block),
            step(HEAD_DIM, block),
            step(1, block),
            step(2, block),
        ],
        out_specs=[pl.BlockSpec((3 * block, HEAD_DIM), lambda i: (0, 0))] * n,
        scratch_shapes=[
            pltpu.VMEM((n, rows, HEAD_DIM), BF16),
            pltpu.VMEM((n, block, HEAD_DIM), BF16),
            pltpu.VMEM((n, HEAD_DIM, block), BF16),
            pltpu.VMEM((n, block, HEAD_DIM), BF16),
            pltpu.VMEM((n, block, HEAD_DIM), F32),
            pltpu.VMEM((n, block, HEAD_DIM), F32),
            pltpu.VMEM((HEAD_DIM, block), F32),
            pltpu.SMEM((3,), jnp.int32),
            pltpu.SemaphoreType.DMA((n,)),
            pltpu.SemaphoreType.DMA((n,)),
        ],
        compiler_params=params,
        name="backward",
    )(rank, *a, *g, probs, out_t, inv_total, stats_by_block)
    back = [swap(grads[m], m) for m in range(n)]
    grad_outs = pl.pallas_call(
        functools.partial(unpack_kernel, block),
        out_shape=[shape_of((block, width_dev), BF16)] * 3,
        in_specs=[SMEM_SPEC] + [ANY_SPEC] * n,
        out_specs=[ANY_SPEC] * 3,
        scratch_shapes=[pltpu.SemaphoreType.DMA((3 * n,))],
        name="unpack",
    )(rank, *back)
    return (normed, *grad_outs)


def from_behind(value, axis, steps):
    count = lax.axis_size(axis)
    initial, last = (max(0, -steps), min(count, count - steps))
    return lax.ppermute(value, axis, [(source, source + steps) for source in range(initial, last)])


def allowed_pairs(all_docs, own_docs, query_pos, seq_rank, offset, block_len):
    key_start = (seq_rank - offset) * block_len
    key_pos = key_start + jnp.arange(block_len, dtype=jnp.int32)
    key_docs = lax.dynamic_slice_in_dim(all_docs, jnp.maximum(key_start, 0), block_len)
    return (
        (key_pos[None, :] >= 0)
        & (key_pos[None, :] <= query_pos[:, None])
        & (key_docs[None, :] == own_docs[:, None])
    )


def masked_scores(query_heads, source, allowed, score_scale):
    key_heads = source[0].reshape(query_heads.shape)
    scores = (
        jnp.einsum("qhd,khd->hqk", query_heads, key_heads, preferred_element_type=jnp.float32)
        * score_scale
    )
    return jnp.where(allowed[None], scores, -jnp.inf)


def by_block(queries, keys, values, grad_normed, docs):
    block_len, width_dev = queries.shape
    heads_dev = width_dev // HEAD_DIM
    width = HEADS * HEAD_DIM
    score_scale = 1.0 / math.sqrt(HEAD_DIM)
    seq_rank = lax.axis_index("seq")
    levels = lax.axis_size("seq").bit_length() - 1
    distances = [2**exponent for exponent in range(levels)]
    all_docs = lax.all_gather(docs, "seq", axis=0, tiled=True)
    query_pos = seq_rank * block_len + jnp.arange(block_len, dtype=jnp.int32)
    query_heads = queries.reshape(block_len, heads_dev, HEAD_DIM)
    key_value = jnp.stack([keys, values])
    fetched = [from_behind(key_value, "seq", offset) for offset in distances]
    offsets = [0] + distances
    sources = [key_value] + fetched
    masks = [
        allowed_pairs(all_docs, docs, query_pos, seq_rank, offset, block_len) for offset in offsets
    ]
    shape_heads = (block_len, heads_dev, HEAD_DIM)
    row_max = jnp.full((heads_dev, block_len), -jnp.inf, jnp.float32)
    row_sum = jnp.zeros((heads_dev, block_len), jnp.float32)
    for source, allowed in zip(sources, masks):

        def update_stats(state, source_kv, allowed_now):
            old_max, old_sum = state
            scores = masked_scores(query_heads, source_kv, allowed_now, score_scale)
            new_max = jnp.maximum(old_max, jnp.max(scores, axis=-1))
            new_sum = old_sum * jnp.exp(old_max - new_max) + jnp.sum(
                jnp.exp(scores - new_max[..., None]), axis=-1
            )
            return (new_max, new_sum)

        def keep_stats(state, source_kv, allowed_now):
            return state

        row_max, row_sum = lax.cond(
            jnp.any(allowed), update_stats, keep_stats, (row_max, row_sum), source, allowed
        )
    log_total = row_max + jnp.log(row_sum)
    attn = jnp.zeros(shape_heads, jnp.float32)
    for source, allowed in zip(sources, masks):

        def forward_term(source_kv, allowed_now):
            scores = masked_scores(query_heads, source_kv, allowed_now, score_scale)
            prob_round = jnp.exp(scores - log_total[..., None]).astype(jnp.bfloat16)
            value_heads = source_kv[1].reshape(shape_heads)
            return jnp.einsum(
                "hqk,khd->qhd", prob_round, value_heads, preferred_element_type=jnp.float32
            )

        def empty_term(source_kv, allowed_now):
            return jnp.zeros(shape_heads, jnp.float32)

        attn = attn + lax.cond(jnp.any(allowed), forward_term, empty_term, source, allowed)
    attn_flat = attn.reshape(block_len, width_dev)
    cotangent = grad_normed.astype(jnp.float32)
    square_local = jnp.sum(attn_flat * attn_flat, axis=-1)
    square_total = lax.psum(square_local, "head")
    inv_rms = lax.rsqrt(square_total / width + norm_eps)
    normed = (attn_flat * inv_rms[:, None]).astype(jnp.bfloat16)
    projection = lax.psum(jnp.sum(cotangent * attn_flat, axis=-1), "head")
    dattn = (
        inv_rms[:, None] * cotangent - attn_flat * (inv_rms**3 * projection / width)[:, None]
    ).astype(jnp.bfloat16)
    dattn_heads = dattn.reshape(shape_heads)
    row_delta = jnp.sum(dattn_heads.astype(jnp.float32) * attn, axis=-1).T
    grad_query = jnp.zeros(shape_heads, jnp.float32)
    partials = []
    for source, allowed in zip(sources, masks):

        def backward_term(source_kv, allowed_now):
            scores = masked_scores(query_heads, source_kv, allowed_now, score_scale)
            prob_exact = jnp.exp(scores - log_total[..., None])
            prob_round = prob_exact.astype(jnp.bfloat16)
            key_heads = source_kv[0].reshape(shape_heads)
            value_heads = source_kv[1].reshape(shape_heads)
            dprob = jnp.einsum(
                "qhd,khd->hqk", dattn_heads, value_heads, preferred_element_type=jnp.float32
            )
            dscore = (prob_exact * (dprob - row_delta[..., None]) * score_scale).astype(
                jnp.bfloat16
            )
            query_term = jnp.einsum(
                "hqk,khd->qhd", dscore, key_heads, preferred_element_type=jnp.float32
            )
            key_term = jnp.einsum(
                "hqk,qhd->khd", dscore, query_heads, preferred_element_type=jnp.float32
            )
            value_term = jnp.einsum(
                "hqk,qhd->khd", prob_round, dattn_heads, preferred_element_type=jnp.float32
            )
            return (
                query_term,
                jnp.stack(
                    [
                        key_term.reshape(block_len, width_dev),
                        value_term.reshape(block_len, width_dev),
                    ]
                ),
            )

        def empty_pair(source_kv, allowed_now):
            return (
                jnp.zeros(shape_heads, jnp.float32),
                jnp.zeros((2, block_len, width_dev), jnp.float32),
            )

        query_term, pair_term = lax.cond(
            jnp.any(allowed), backward_term, empty_pair, source, allowed
        )
        grad_query = grad_query + query_term
        partials.append(pair_term)
    local_term = partials[0]
    far_terms = partials[1:]
    summed = local_term
    for offset, addend in zip(distances, far_terms):
        summed = summed + from_behind(addend.astype(jnp.bfloat16), "seq", -offset).astype(
            addend.dtype
        )
    grad_queries = grad_query.reshape(block_len, width_dev).astype(jnp.bfloat16)
    return (normed, grad_queries, summed[0].astype(jnp.bfloat16), summed[1].astype(jnp.bfloat16))


def body(queries, *others):
    block_len, width_dev = queries.shape
    if lax.axis_size("seq") == 8 and width_dev == 8 * HEAD_DIM and block_len == 512:
        return by_head(queries, *others)
    return by_block(queries, *others)


def solution(mesh):
    placed = (P("seq", "head"), P("seq", "head"), P("seq", "head"), P("seq", "head"), P("seq"))
    return jax.shard_map(
        body,
        mesh=mesh,
        in_specs=placed,
        out_specs=(P("seq", "head"), P("seq", "head"), P("seq", "head"), P("seq", "head")),
        check_vma=False,
    )
```

profile of v0, /device:TPU:0, one launch (start us, length us, event | category | flops | bytes accessed | tf_op | source)
XLA Modules:
  0.0 410.1 jit_solution(388929538286981951)
XLA Ops:
  0.6 0.7 convert_bitcast_fusion
  1.9 129.5 %pack.1 = (bf16[1552,128]{1,0:T(8,128)(2,1)}, bf16[1552,128]{1,0:T(8,128)(2,1)}, bf16[1552,128]{1,0:T(8,128)(2,1)}, bf16[1552,128]{1,0:T(8,128)(2,1)}, bf16[1552...) custom-call(s32[1]{0:T(128)} %bitcast.rank_ref, ...), custom_call_target="tpu_custom_call" | custom-call | tf_op jit(solution)/shard_map/pack/pallas_call | solution.py:302
  132.0 2.6 collective-permute-start.8
  135.0 1.4 collective-permute-start.9
  136.4 1.5 collective-permute-start.10
  137.9 9.7 %collective-permute-done.1.refs_2_.refs_10_ = bf16[512,128]{1,0:T(8,128)(2,1)S(1)} collective-permute-done((bf16[512,128]{1,0:T(8,128)(2,1)}, bf16[512,128]{1,0:T(8,128)(2,1)S(1)}, u32[]{:S(2)}, u32[]{:S(2)}) %collective-permute-start.1) | collective-permute-done | bytes 131104 | tf_op jit(solution)/shard_map/ppermute | solution.py:278
  147.6 0.8 collective-permute-start.11
  148.4 2.2 collective-permute-start.12
  150.6 1.4 collective-permute-start.13
  151.9 3.7 collective-permute-done.9.refs_3_
  155.7 2.1 collective-permute-start.2
  157.8 1.5 collective-permute-start.3
  159.3 16.6 %collective-permute-done.11.refs_5_ = bf16[1552,128]{1,0:T(8,128)(2,1)S(1)} collective-permute-done((bf16[1552,128]{1,0:T(8,128)(2,1)}, bf16[1552,128]{1,0:T(8,128)(2,1)S(1)}, u32[]{:S(2)}, u32[]{:S(2)}) %collective-permute-start.11) | collective-permute-done | bytes 397344 | tf_op jit(solution)/shard_map/ppermute | solution.py:278
  175.9 1.0 collective-permute-start.4
  176.9 2.5 collective-permute-start.5
  179.4 1.2 collective-permute-start.6
  180.7 20.1 %forward.1 = (bf16[8,4,512,512]{3,2,1,0:T(8,128)(2,1)}, f32[8,128,512]{2,1,0:T(8,128)}, bf16[8,512,128]{2,1,0:T(8,128)(2,1)}, f32[8,1,512]{2,1,0:T(1,128)}, f32[8,1,512]{2,1,0:T(1,128)}) custom-call(s32[1]{0:T(128)} %bitcast.rank_ref, bf16[1552,128]{1,0:T(8,128)(2,1)} %get-tuple-element.44.refs_0_, bf16[1552,128]{1,0:T(8,128)(2,1)} %copy-done, ...), custom_call_target="tpu_custom_call" | custom-call | tf_op jit(solution)/shard_map/forward/pallas_call | solution.py:314
  201.7 3.9 project.1
  205.7 1.4 collective-permute-done.14
  207.1 0.8 add.49
  207.9 1.5 collective-permute-start.17
  209.4 1.5 collective-permute-start.16
  211.5 1.3 collective-permute-done.17
  213.3 1.5 collective-permute-done.15
  214.9 3.6 collective-permute-start.20
  218.5 1.0 collective-permute-start.18
  219.5 2.0 dynamic-slice_bitcast_fusion
  221.6 1.8 collective-permute-done.19
  223.3 0.9 collective-permute-done.18
  224.9 26.4 %backward.1 = (bf16[1536,128]{1,0:T(8,128)(2,1)}, bf16[1536,128]{1,0:T(8,128)(2,1)}, bf16[1536,128]{1,0:T(8,128)(2,1)}, bf16[1536,128]{1,0:T(8,128)(2,1)}, bf16[...) custom-call(s32[1]{0:T(128)} %bitcast.rank_ref, ...), custom_call_target="tpu_custom_call" | custom-call | tf_op jit(solution)/shard_map/backward/pallas_call | solution.py:374
  251.9 1.5 collective-permute-start.22
  253.5 0.7 collective-permute-start.24
  254.2 12.1 %collective-permute-done.22.refs_2_ = bf16[512,128]{1,0:T(8,128)(2,1)S(1)} collective-permute-done((bf16[512,128]{1,0:T(8,128)(2,1)S(1)}, bf16[512,128]{1,0:T(8,128)(2,1)S(1)}, u32[]{:S(2)}, u32[]{:S(2)}) %collective-permute-start.22) | collective-permute-done | bytes 131104 | tf_op jit(solution)/shard_map/ppermute | solution.py:278
  266.3 1.9 collective-permute-done.23.refs_3_
  268.2 0.7 collective-permute-start.26
  269.0 1.8 collective-permute-start.27
  270.8 0.8 collective-permute-done.25.refs_5_
  271.5 3.9 collective-permute-done.26.refs_6_
  276.1 0.9 collective-permute-done.27.refs_7_
  277.0 1.3 collective-permute-start.32
  278.3 0.8 collective-permute-start.33
  279.1 1.6 collective-permute-start.34
  280.7 1.3 dynamic-slice_bitcast_fusion.8.stats_ref
  282.1 2.7 normed.1
  284.8 19.7 %collective-permute-done.31.refs_4_ = bf16[1536,128]{1,0:T(8,128)(2,1)S(1)} collective-permute-done((bf16[1536,128]{1,0:T(8,128)(2,1)}, bf16[1536,128]{1,0:T(8,128)(2,1)S(1)}, u32[]{:S(2)}, u32[]{:S(2)}) %collective-permute-start.31) | collective-permute-done | bytes 393248 | tf_op jit(solution)/shard_map/ppermute | solution.py:278
  304.5 7.9 %collective-permute-done.32.refs_5_ = bf16[1536,128]{1,0:T(8,128)(2,1)S(1)} collective-permute-done((bf16[1536,128]{1,0:T(8,128)(2,1)}, bf16[1536,128]{1,0:T(8,128)(2,1)S(1)}, u32[]{:S(2)}, u32[]{:S(2)}) %collective-permute-start.32) | collective-permute-done | bytes 393248 | tf_op jit(solution)/shard_map/ppermute | solution.py:278
  312.5 0.7 copy-done.18
  313.5 96.6 %unpack.1 = (bf16[512,1024]{1,0:T(8,128)(2,1)}, bf16[512,1024]{1,0:T(8,128)(2,1)}, bf16[512,1024]{1,0:T(8,128)(2,1)}) custom-call(s32[1]{0:T(128)} %bitcast.rank_ref, bf16[1536,128]{1,0:T(8,128)(2,1)} %get-tuple-element.57.refs_0_, bf16[1536,128]{1,0:T(8,128)(2,1)} %copy-done.14, bf16[1536,128]{1,0:T(8,128)(2,1)} %copy-done.15, ...), custom_call_target="tpu_custom_call" | custom-call | tf_op jit(solution)/shard_map/unpack/pallas_call | solution.py:401
  (91 shorter events, 6.0 us)
Async XLA Ops:
  131.4 17.0 %collective-permute-start.7 = (bf16[1552,128]{1,0:T(8,128)(2,1)}, bf16[1552,128]{1,0:T(8,128)(2,1)S(1)}, u32[]{:S(2)}, u32[]{:S(2)}) collective-permute-start(bf16[1552,128]{1,0:T(8,128)(2,1)} %get-tuple-element.45), channel_id=1, source_target_pairs={{0,4},{4,0},{8,12},{12,8},{16,20},{20,16},{24,28},{28,24},{1,5},{5... | collective-permute-start | bytes 1191944 | tf_op jit(solution)/shard_map/ppermute | solution.py:278
  132.0 18.6 %collective-permute-start.8 = (bf16[1552,128]{1,0:T(8,128)(2,1)}, bf16[1552,128]{1,0:T(8,128)(2,1)S(1)}, u32[]{:S(2)}, u32[]{:S(2)}) collective-permute-start(bf16[1552,128]{1,0:T(8,128)(2,1)} %get-tuple-element.46), channel_id=1, source_target_pairs={{0,8},{4,12},{8,0},{12,4},{16,24},{20,28},{24,16},{28,20},{1,9},{5... | collective-permute-start | bytes 1191944 | tf_op jit(solution)/shard_map/ppermute | solution.py:278
  134.5 1.9 collective-permute-start
  134.7 12.9 %collective-permute-start.1 = (bf16[512,128]{1,0:T(8,128)(2,1)}, bf16[512,128]{1,0:T(8,128)(2,1)S(1)}, u32[]{:S(2)}, u32[]{:S(2)}) collective-permute-start(bf16[512,128]{1,0:T(8,128)(2,1)} %get-tuple-element.38), channel_id=1, source_target_pairs={{0,8},{4,12},{8,0},{12,4},{16,24},{20,28},{24,16},{28,20},{1,9},{5... | collective-permute-start | bytes 393224 | tf_op jit(solution)/shard_map/ppermute | solution.py:278
  135.0 20.7 %collective-permute-start.9 = (bf16[1552,128]{1,0:T(8,128)(2,1)}, bf16[1552,128]{1,0:T(8,128)(2,1)S(1)}, u32[]{:S(2)}, u32[]{:S(2)}) collective-permute-start(bf16[1552,128]{1,0:T(8,128)(2,1)} %get-tuple-element.47), channel_id=1, source_target_pairs={{0,12},{4,8},{8,4},{12,0},{16,28},{20,24},{24,20},{28,16},{1,13},{... | collective-permute-start | bytes 1191944 | tf_op jit(solution)/shard_map/ppermute | solution.py:278
  136.4 64.5 %copy-start.7 = (bf16[512,128]{1,0:T(8,128)(2,1)}, bf16[512,128]{1,0:T(8,128)(2,1)S(1)}, u32[]{:S(2)}) copy-start(bf16[512,128]{1,0:T(8,128)(2,1)S(1)} %collective-permute-done.refs_1_.refs_9_) | copy-start | bytes 393220
  136.4 21.4 %collective-permute-start.10 = (bf16[1552,128]{1,0:T(8,128)(2,1)}, bf16[1552,128]{1,0:T(8,128)(2,1)S(1)}, u32[]{:S(2)}, u32[]{:S(2)}) collective-permute-start(bf16[1552,128]{1,0:T(8,128)(2,1)} %get-tuple-element.48), channel_id=1, source_target_pairs={{0,16},{4,20},{8,24},{12,28},{16,0},{20,4},{24,8},{28,12},{1,17},{... | collective-permute-start | bytes 1191944 | tf_op jit(solution)/shard_map/ppermute | solution.py:278
  147.6 53.3 %copy-start.8 = (bf16[512,128]{1,0:T(8,128)(2,1)}, bf16[512,128]{1,0:T(8,128)(2,1)S(1)}, u32[]{:S(2)}) copy-start(bf16[512,128]{1,0:T(8,128)(2,1)S(1)} %collective-permute-done.1.refs_2_.refs_10_) | copy-start | bytes 393220
  147.6 28.3 %collective-permute-start.11 = (bf16[1552,128]{1,0:T(8,128)(2,1)}, bf16[1552,128]{1,0:T(8,128)(2,1)S(1)}, u32[]{:S(2)}, u32[]{:S(2)}) collective-permute-start(bf16[1552,128]{1,0:T(8,128)(2,1)} %get-tuple-element.49), channel_id=1, source_target_pairs={{0,20},{4,16},{8,28},{12,24},{16,4},{20,0},{24,12},{28,8},{1,21},{... | collective-permute-start | bytes 1191944 | tf_op jit(solution)/shard_map/ppermute | solution.py:278
  148.4 32.2 %copy-start = (bf16[1552,128]{1,0:T(8,128)(2,1)}, bf16[1552,128]{1,0:T(8,128)(2,1)S(1)}, u32[]{:S(2)}) copy-start(bf16[1552,128]{1,0:T(8,128)(2,1)S(1)} %collective-permute-done.7.refs_1_) | copy-start | bytes 1191940
  148.4 28.5 %collective-permute-start.12 = (bf16[1552,128]{1,0:T(8,128)(2,1)}, bf16[1552,128]{1,0:T(8,128)(2,1)S(1)}, u32[]{:S(2)}, u32[]{:S(2)}) collective-permute-start(bf16[1552,128]{1,0:T(8,128)(2,1)} %get-tuple-element.50), channel_id=1, source_target_pairs={{0,24},{4,28},{8,16},{12,20},{16,8},{20,12},{24,0},{28,4},{1,25},{... | collective-permute-start | bytes 1191944 | tf_op jit(solution)/shard_map/ppermute | solution.py:278
  150.6 30.1 %copy-start.1 = (bf16[1552,128]{1,0:T(8,128)(2,1)}, bf16[1552,128]{1,0:T(8,128)(2,1)S(1)}, u32[]{:S(2)}) copy-start(bf16[1552,128]{1,0:T(8,128)(2,1)S(1)} %collective-permute-done.8.refs_2_) | copy-start | bytes 1191940
  150.6 28.8 %collective-permute-start.13 = (bf16[1552,128]{1,0:T(8,128)(2,1)}, bf16[1552,128]{1,0:T(8,128)(2,1)S(1)}, u32[]{:S(2)}, u32[]{:S(2)}) collective-permute-start(bf16[1552,128]{1,0:T(8,128)(2,1)} %get-tuple-element.51), channel_id=1, source_target_pairs={{0,28},{4,24},{8,20},{12,16},{16,12},{20,8},{24,4},{28,0},{1,29},{... | collective-permute-start | bytes 1191944 | tf_op jit(solution)/shard_map/ppermute | solution.py:278
  155.7 25.0 %copy-start.2 = (bf16[1552,128]{1,0:T(8,128)(2,1)}, bf16[1552,128]{1,0:T(8,128)(2,1)S(1)}, u32[]{:S(2)}) copy-start(bf16[1552,128]{1,0:T(8,128)(2,1)S(1)} %collective-permute-done.9.refs_3_) | copy-start | bytes 1191940
  155.7 45.1 %collective-permute-start.2 = (bf16[512,128]{1,0:T(8,128)(2,1)}, bf16[512,128]{1,0:T(8,128)(2,1)S(1)}, u32[]{:S(2)}, u32[]{:S(2)}) collective-permute-start(bf16[512,128]{1,0:T(8,128)(2,1)} %get-tuple-element.39), channel_id=1, source_target_pairs={{0,12},{4,8},{8,4},{12,0},{16,28},{20,24},{24,20},{28,16},{1,13},{... | collective-permute-start | bytes 393224 | tf_op jit(solution)/shard_map/ppermute | solution.py:278
  157.8 22.9 %copy-start.3 = (bf16[1552,128]{1,0:T(8,128)(2,1)}, bf16[1552,128]{1,0:T(8,128)(2,1)S(1)}, u32[]{:S(2)}) copy-start(bf16[1552,128]{1,0:T(8,128)(2,1)S(1)} %collective-permute-done.10.refs_4_) | copy-start | bytes 1191940
  157.8 43.0 %collective-permute-start.3 = (bf16[512,128]{1,0:T(8,128)(2,1)}, bf16[512,128]{1,0:T(8,128)(2,1)S(1)}, u32[]{:S(2)}, u32[]{:S(2)}) collective-permute-start(bf16[512,128]{1,0:T(8,128)(2,1)} %get-tuple-element.40), channel_id=1, source_target_pairs={{0,16},{4,20},{8,24},{12,28},{16,0},{20,4},{24,8},{28,12},{1,17},{... | collective-permute-start | bytes 393224 | tf_op jit(solution)/shard_map/ppermute | solution.py:278
  175.9 25.0 %collective-permute-start.4 = (bf16[512,128]{1,0:T(8,128)(2,1)}, bf16[512,128]{1,0:T(8,128)(2,1)S(1)}, u32[]{:S(2)}, u32[]{:S(2)}) collective-permute-start(bf16[512,128]{1,0:T(8,128)(2,1)} %get-tuple-element.41), channel_id=1, source_target_pairs={{0,20},{4,16},{8,28},{12,24},{16,4},{20,0},{24,12},{28,8},{1,21},{... | collective-permute-start | bytes 393224 | tf_op jit(solution)/shard_map/ppermute | solution.py:278
  176.9 24.0 %collective-permute-start.5 = (bf16[512,128]{1,0:T(8,128)(2,1)}, bf16[512,128]{1,0:T(8,128)(2,1)S(1)}, u32[]{:S(2)}, u32[]{:S(2)}) collective-permute-start(bf16[512,128]{1,0:T(8,128)(2,1)} %get-tuple-element.42), channel_id=1, source_target_pairs={{0,24},{4,28},{8,16},{12,20},{16,8},{20,12},{24,0},{28,4},{1,25},{... | collective-permute-start | bytes 393224 | tf_op jit(solution)/shard_map/ppermute | solution.py:278
  179.4 21.5 %collective-permute-start.6 = (bf16[512,128]{1,0:T(8,128)(2,1)}, bf16[512,128]{1,0:T(8,128)(2,1)S(1)}, u32[]{:S(2)}, u32[]{:S(2)}) collective-permute-start(bf16[512,128]{1,0:T(8,128)(2,1)} %get-tuple-element.43), channel_id=1, source_target_pairs={{0,28},{4,24},{8,20},{12,16},{16,12},{20,8},{24,4},{28,0},{1,29},{... | collective-permute-start | bytes 393224 | tf_op jit(solution)/shard_map/ppermute | solution.py:278
  205.6 1.5 collective-permute-start.14
  207.9 4.9 %collective-permute-start.17 = (f32[2,4096]{1,0:T(2,128)S(1)}, f32[2,4096]{1,0:T(2,128)S(1)}, u32[]{:S(2)}, u32[]{:S(2)}) collective-permute-start(f32[2,4096]{1,0:T(2,128)S(1)} %add.49), channel_id=1, source_target_pairs={{0,24},{4,28},{8,16},{12,20},{16,8},{20,12},{24,0},{28,4},{1,25},{... | collective-permute-start | bytes 98312 | tf_op jit(solution)/shard_map/ppermute | solution.py:278
  209.4 3.9 collective-permute-start.16
  210.9 3.9 collective-permute-start.15
  214.9 6.7 %collective-permute-start.20 = (f32[2,4096]{1,0:T(2,128)S(1)}, f32[2,4096]{1,0:T(2,128)S(1)}, u32[]{:S(2)}, u32[]{:S(2)}) collective-permute-start(f32[2,4096]{1,0:T(2,128)S(1)} %add_add_fusion.1), channel_id=1, source_target_pairs={{0,3},{1,0},{2,1},{3,2},{4,7},{5,4},{6,5},{7,6},{8,11},{9,8},{10,9... | collective-permute-start | bytes 98312 | tf_op jit(solution)/shard_map/ppermute | solution.py:286
  218.5 4.8 %collective-permute-start.19 = (f32[2,4096]{1,0:T(2,128)S(1)}, f32[2,4096]{1,0:T(2,128)S(1)}, u32[]{:S(2)}, u32[]{:S(2)}) collective-permute-start(f32[2,4096]{1,0:T(2,128)S(1)} %add_add_fusion.1), channel_id=1, source_target_pairs={{0,2},{1,3},{2,0},{3,1},{4,6},{5,7},{6,4},{7,5},{8,10},{9,11},{10,... | collective-permute-start | bytes 98312 | tf_op jit(solution)/shard_map/ppermute | solution.py:286
  218.5 5.7 %collective-permute-start.18 = (f32[2,4096]{1,0:T(2,128)S(1)}, f32[2,4096]{1,0:T(2,128)S(1)}, u32[]{:S(2)}, u32[]{:S(2)}) collective-permute-start(f32[2,4096]{1,0:T(2,128)S(1)} %add_add_fusion.1), channel_id=1, source_target_pairs={{0,1},{1,2},{2,3},{3,0},{4,5},{5,6},{6,7},{7,4},{8,9},{9,10},{10,1... | collective-permute-start | bytes 98312 | tf_op jit(solution)/shard_map/ppermute | solution.py:286
  221.6 31.9 %collective-permute-start.21 = (bf16[512,128]{1,0:T(8,128)(2,1)S(1)}, bf16[512,128]{1,0:T(8,128)(2,1)S(1)}, u32[]{:S(2)}, u32[]{:S(2)}) collective-permute-start(bf16[512,128]{1,0:T(8,128)(2,1)S(1)} %get-tuple-element.74), channel_id=1, source_target_pairs={{0,4},{4,0},{8,12},{12,8},{16,20},{20,16},{24,28},{28,24},{1,5},{5... | collective-permute-start | bytes 393224 | tf_op jit(solution)/shard_map/ppermute | solution.py:278
  251.2 27.0 %collective-permute-start.28 = (bf16[1536,128]{1,0:T(8,128)(2,1)}, bf16[1536,128]{1,0:T(8,128)(2,1)S(1)}, u32[]{:S(2)}, u32[]{:S(2)}) collective-permute-start(bf16[1536,128]{1,0:T(8,128)(2,1)} %get-tuple-element.58), channel_id=1, source_target_pairs={{0,4},{4,0},{8,12},{12,8},{16,20},{20,16},{24,28},{28,24},{1,5},{5... | collective-permute-start | bytes 1179656 | tf_op jit(solution)/shard_map/ppermute | solution.py:278
  251.3 27.8 %collective-permute-start.29 = (bf16[1536,128]{1,0:T(8,128)(2,1)}, bf16[1536,128]{1,0:T(8,128)(2,1)S(1)}, u32[]{:S(2)}, u32[]{:S(2)}) collective-permute-start(bf16[1536,128]{1,0:T(8,128)(2,1)} %get-tuple-element.59), channel_id=1, source_target_pairs={{0,8},{4,12},{8,0},{12,4},{16,24},{20,28},{24,16},{28,20},{1,9},{5... | collective-permute-start | bytes 1179656 | tf_op jit(solution)/shard_map/ppermute | solution.py:278
  251.9 14.4 %collective-permute-start.22 = (bf16[512,128]{1,0:T(8,128)(2,1)S(1)}, bf16[512,128]{1,0:T(8,128)(2,1)S(1)}, u32[]{:S(2)}, u32[]{:S(2)}) collective-permute-start(bf16[512,128]{1,0:T(8,128)(2,1)S(1)} %get-tuple-element.73), channel_id=1, source_target_pairs={{0,8},{4,12},{8,0},{12,4},{16,24},{20,28},{24,16},{28,20},{1,9},{5... | collective-permute-start | bytes 393224 | tf_op jit(solution)/shard_map/ppermute | solution.py:278
  253.4 14.8 %collective-permute-start.23 = (bf16[512,128]{1,0:T(8,128)(2,1)S(1)}, bf16[512,128]{1,0:T(8,128)(2,1)S(1)}, u32[]{:S(2)}, u32[]{:S(2)}) collective-permute-start(bf16[512,128]{1,0:T(8,128)(2,1)S(1)} %get-tuple-element.72), channel_id=1, source_target_pairs={{0,12},{4,8},{8,4},{12,0},{16,28},{20,24},{24,20},{28,16},{1,13},{... | collective-permute-start | bytes 393224 | tf_op jit(solution)/shard_map/ppermute | solution.py:278
  253.5 28.6 %copy-start.21 = (bf16[512,128]{1,0:T(8,128)(2,1)}, bf16[512,128]{1,0:T(8,128)(2,1)S(1)}, u32[]{:S(2)}) copy-start(bf16[512,128]{1,0:T(8,128)(2,1)S(1)} %collective-permute-done.21.refs_1_) | copy-start | bytes 393220
  253.5 15.5 %collective-permute-start.24 = (bf16[512,128]{1,0:T(8,128)(2,1)S(1)}, bf16[512,128]{1,0:T(8,128)(2,1)S(1)}, u32[]{:S(2)}, u32[]{:S(2)}) collective-permute-start(bf16[512,128]{1,0:T(8,128)(2,1)S(1)} %get-tuple-element.71), channel_id=1, source_target_pairs={{0,16},{4,20},{8,24},{12,28},{16,0},{20,4},{24,8},{28,12},{1,17},{... | collective-permute-start | bytes 393224 | tf_op jit(solution)/shard_map/ppermute | solution.py:278
  266.3 15.7 %copy-start.22 = (bf16[512,128]{1,0:T(8,128)(2,1)}, bf16[512,128]{1,0:T(8,128)(2,1)S(1)}, u32[]{:S(2)}) copy-start(bf16[512,128]{1,0:T(8,128)(2,1)S(1)} %collective-permute-done.22.refs_2_) | copy-start | bytes 393220
  266.3 5.2 %collective-permute-start.25 = (bf16[512,128]{1,0:T(8,128)(2,1)S(1)}, bf16[512,128]{1,0:T(8,128)(2,1)S(1)}, u32[]{:S(2)}, u32[]{:S(2)}) collective-permute-start(bf16[512,128]{1,0:T(8,128)(2,1)S(1)} %get-tuple-element.70), channel_id=1, source_target_pairs={{0,20},{4,16},{8,28},{12,24},{16,4},{20,0},{24,12},{28,8},{1,21},{... | collective-permute-start | bytes 393224 | tf_op jit(solution)/shard_map/ppermute | solution.py:278
  268.2 13.8 %copy-start.23 = (bf16[512,128]{1,0:T(8,128)(2,1)}, bf16[512,128]{1,0:T(8,128)(2,1)S(1)}, u32[]{:S(2)}) copy-start(bf16[512,128]{1,0:T(8,128)(2,1)S(1)} %collective-permute-done.23.refs_3_) | copy-start | bytes 393220
  268.2 7.2 %collective-permute-start.26 = (bf16[512,128]{1,0:T(8,128)(2,1)S(1)}, bf16[512,128]{1,0:T(8,128)(2,1)S(1)}, u32[]{:S(2)}, u32[]{:S(2)}) collective-permute-start(bf16[512,128]{1,0:T(8,128)(2,1)S(1)} %get-tuple-element.69), channel_id=1, source_target_pairs={{0,24},{4,28},{8,16},{12,20},{16,8},{20,12},{24,0},{28,4},{1,25},{... | collective-permute-start | bytes 393224 | tf_op jit(solution)/shard_map/ppermute | solution.py:278
  269.0 13.1 %copy-start.24 = (bf16[512,128]{1,0:T(8,128)(2,1)}, bf16[512,128]{1,0:T(8,128)(2,1)S(1)}, u32[]{:S(2)}) copy-start(bf16[512,128]{1,0:T(8,128)(2,1)S(1)} %collective-permute-done.24.refs_4_) | copy-start | bytes 393220
  269.0 8.0 %collective-permute-start.27 = (bf16[512,128]{1,0:T(8,128)(2,1)S(1)}, bf16[512,128]{1,0:T(8,128)(2,1)S(1)}, u32[]{:S(2)}, u32[]{:S(2)}) collective-permute-start(bf16[512,128]{1,0:T(8,128)(2,1)S(1)} %get-tuple-element.68), channel_id=1, source_target_pairs={{0,28},{4,24},{8,20},{12,16},{16,12},{20,8},{24,4},{28,0},{1,29},{... | collective-permute-start | bytes 393224 | tf_op jit(solution)/shard_map/ppermute | solution.py:278
  271.5 13.3 %collective-permute-start.30 = (bf16[1536,128]{1,0:T(8,128)(2,1)}, bf16[1536,128]{1,0:T(8,128)(2,1)S(1)}, u32[]{:S(2)}, u32[]{:S(2)}) collective-permute-start(bf16[1536,128]{1,0:T(8,128)(2,1)} %get-tuple-element.60), channel_id=1, source_target_pairs={{0,12},{4,8},{8,4},{12,0},{16,28},{20,24},{24,20},{28,16},{1,13},{... | collective-permute-start | bytes 1179656 | tf_op jit(solution)/shard_map/ppermute | solution.py:278
  275.4 29.1 %collective-permute-start.31 = (bf16[1536,128]{1,0:T(8,128)(2,1)}, bf16[1536,128]{1,0:T(8,128)(2,1)S(1)}, u32[]{:S(2)}, u32[]{:S(2)}) collective-permute-start(bf16[1536,128]{1,0:T(8,128)(2,1)} %get-tuple-element.61), channel_id=1, source_target_pairs={{0,16},{4,20},{8,24},{12,28},{16,0},{20,4},{24,8},{28,12},{1,17},{... | collective-permute-start | bytes 1179656 | tf_op jit(solution)/shard_map/ppermute | solution.py:278
  277.0 35.4 %collective-permute-start.32 = (bf16[1536,128]{1,0:T(8,128)(2,1)}, bf16[1536,128]{1,0:T(8,128)(2,1)S(1)}, u32[]{:S(2)}, u32[]{:S(2)}) collective-permute-start(bf16[1536,128]{1,0:T(8,128)(2,1)} %get-tuple-element.62), channel_id=1, source_target_pairs={{0,20},{4,16},{8,28},{12,24},{16,4},{20,0},{24,12},{28,8},{1,21},{... | collective-permute-start | bytes 1179656 | tf_op jit(solution)/shard_map/ppermute | solution.py:278
  278.3 34.2 %copy-start.14 = (bf16[1536,128]{1,0:T(8,128)(2,1)}, bf16[1536,128]{1,0:T(8,128)(2,1)S(1)}, u32[]{:S(2)}) copy-start(bf16[1536,128]{1,0:T(8,128)(2,1)S(1)} %collective-permute-done.28.refs_1_) | copy-start | bytes 1179652
  278.3 34.1 %collective-permute-start.33 = (bf16[1536,128]{1,0:T(8,128)(2,1)}, bf16[1536,128]{1,0:T(8,128)(2,1)S(1)}, u32[]{:S(2)}, u32[]{:S(2)}) collective-permute-start(bf16[1536,128]{1,0:T(8,128)(2,1)} %get-tuple-element.63), channel_id=1, source_target_pairs={{0,24},{4,28},{8,16},{12,20},{16,8},{20,12},{24,0},{28,4},{1,25},{... | collective-permute-start | bytes 1179656 | tf_op jit(solution)/shard_map/ppermute | solution.py:278
  279.1 33.3 %copy-start.15 = (bf16[1536,128]{1,0:T(8,128)(2,1)}, bf16[1536,128]{1,0:T(8,128)(2,1)S(1)}, u32[]{:S(2)}) copy-start(bf16[1536,128]{1,0:T(8,128)(2,1)S(1)} %collective-permute-done.29.refs_2_) | copy-start | bytes 1179652
  279.1 33.3 %collective-permute-start.34 = (bf16[1536,128]{1,0:T(8,128)(2,1)}, bf16[1536,128]{1,0:T(8,128)(2,1)S(1)}, u32[]{:S(2)}, u32[]{:S(2)}) collective-permute-start(bf16[1536,128]{1,0:T(8,128)(2,1)} %get-tuple-element.64), channel_id=1, source_target_pairs={{0,28},{4,24},{8,20},{12,16},{16,12},{20,8},{24,4},{28,0},{1,29},{... | collective-permute-start | bytes 1179656 | tf_op jit(solution)/shard_map/ppermute | solution.py:278
  284.8 27.6 %copy-start.16 = (bf16[1536,128]{1,0:T(8,128)(2,1)}, bf16[1536,128]{1,0:T(8,128)(2,1)S(1)}, u32[]{:S(2)}) copy-start(bf16[1536,128]{1,0:T(8,128)(2,1)S(1)} %collective-permute-done.30.refs_3_) | copy-start | bytes 1179652
  (15 other events, 46.4 us)
where the time goes:
time: 409 us; the launch traced here: 410 us
  Pallas kernels  279 us (68%)
  waiting for transfers between devices  84.6 us (21%)
  starting transfers between devices  37.4 us (9%)
  local copies, waits for them, and re-layouts  5.72 us (1%)
    pallas_call x1, Pallas kernels, by_head(): pl.pallas_call(functools.partial(pack_kernel, block), out_shape=[shape_of...  130 us
    pallas_call x1, Pallas kernels, by_head(): pl.pallas_call(functools.partial(unpack_kernel, block), out_shape=[shape_...  96.6 us
    ppermute x32, waiting for transfers between devices, swap(): return lax.ppermute(value, 'seq', [(s, s ^ m) for s in range(n)])  82 us
    ppermute x32, starting transfers between devices, swap(): return lax.ppermute(value, 'seq', [(s, s ^ m) for s in range(n)])  32.7 us
    pallas_call x1, Pallas kernels, by_head(): pl.pallas_call(functools.partial(backward_kernel, block), grid=(n,), out_...  26.4 us
    pallas_call x1, Pallas kernels, by_head(): pl.pallas_call(functools.partial(forward_kernel, block), grid=(n,), out_s...  20.1 us
  transfers between devices with their start and end apart: 35, of which 16 were waited for; matrix products, arithmetic and copies ran while one was open for 1% of the time, Pallas kernels for 12%

commit v1 on v0

--- a/solution.py
+++ b/solution.py
@@ -303,8 +303,9 @@
         functools.partial(pack_kernel, block),
         out_shape=[shape_of((rows, HEAD_DIM), BF16)] * n + [shape_of((block, HEAD_DIM), BF16)] * n,
         in_specs=[SMEM_SPEC] + [ANY_SPEC] * 5,
-        out_specs=[ANY_SPEC] * (2 * n),
+        out_specs=[VMEM_SPEC] * (2 * n),
         scratch_shapes=[pltpu.SemaphoreType.DMA((5 * n,))],
+        compiler_params=params,
         name="pack",
     )(rank, queries, keys, values, grad_normed, doc_rows)
     a = [swap(packed[m], m) for m in range(n)]
@@ -402,8 +403,9 @@
         functools.partial(unpack_kernel, block),
         out_shape=[shape_of((block, width_dev), BF16)] * 3,
         in_specs=[SMEM_SPEC] + [ANY_SPEC] * n,
-        out_specs=[ANY_SPEC] * 3,
+        out_specs=[VMEM_SPEC] * 3,
         scratch_shapes=[pltpu.SemaphoreType.DMA((3 * n,))],
+        compiler_params=params,
         name="unpack",
     )(rank, *back)
     return (normed, *grad_outs)

time: 409 us -> 193 us (0.47)
  Pallas kernels: 279 us -> 61.7 us
    pallas_call x1, Pallas kernels: 130 us -> 4.76 us  [by_head(): pl.pallas_call(functools.partial(pack_kernel, block), out_shape=[shape_of...]
    pallas_call x1, Pallas kernels: 96.6 us -> 3.78 us  [by_head(): pl.pallas_call(functools.partial(unpack_kernel, block), out_shape=[shape_...]
  transfers between devices with their start and end apart: 35 -> 35, of which waited for: 16 -> 16; matrix products, arithmetic and copies ran while one was open for 1% -> 2% of each run, Pallas kernels for 12% -> 26%
where the time goes in v1:
time: 193 us; the launch traced here: 192 us
  waiting for transfers between devices  84.7 us (44%)
  Pallas kernels  61.7 us (32%)
  starting transfers between devices  37.3 us (19%)
  local copies, waits for them, and re-layouts  5.72 us (3%)
  other arithmetic  2.13 us (1%)
    ppermute x32, waiting for transfers between devices, swap(): return lax.ppermute(value, 'seq', [(s, s ^ m) for s in range(n)])  82 us
    ppermute x32, starting transfers between devices, swap(): return lax.ppermute(value, 'seq', [(s, s ^ m) for s in range(n)])  32.6 us
    pallas_call x1, Pallas kernels, by_head(): pl.pallas_call(functools.partial(backward_kernel, block), grid=(n,), out_...  26.4 us
    pallas_call x1, Pallas kernels, by_head(): pl.pallas_call(functools.partial(forward_kernel, block), grid=(n,), out_s...  20.1 us
    pallas_call x1, Pallas kernels, by_head(): pl.pallas_call(functools.partial(pack_kernel, block), out_shape=[shape_of...  4.76 us
    ppermute x3, starting transfers between devices, sum_everywhere(): lax.ppermute(stats, 'head', [(s, (s + d) % heads) for s in range(heads)])  4.65 us
    pallas_call x1, Pallas kernels, by_head(): pl.pallas_call(functools.partial(project_kernel, block), out_shape=shape_...  3.94 us
  transfers between devices with their start and end apart: 35, of which 16 were waited for; matrix products, arithmetic and copies ran while one was open for 2% of the time, Pallas kernels for 26%

profile of v1, /device:TPU:0, one launch (start us, length us, event | category | flops | bytes accessed | tf_op | source)
XLA Modules:
  0.0 192.5 jit_solution(4973685751566179222)
XLA Ops:
  0.6 0.7 convert_bitcast_fusion
  1.9 4.8 %pack.1 = (bf16[1552,128]{1,0:T(8,128)(2,1)}, bf16[1552,128]{1,0:T(8,128)(2,1)}, bf16[1552,128]{1,0:T(8,128)(2,1)}, bf16[1552,128]{1,0:T(8,128)(2,1)}, bf16[1552...) custom-call(s32[1]{0:T(128)} %bitcast.rank_ref, ...), custom_call_target="tpu_custom_call" | custom-call | tf_op jit(solution)/shard_map/pack/pallas_call | solution.py:302
  7.2 2.6 %collective-permute-start.8 = (bf16[1552,128]{1,0:T(8,128)(2,1)}, bf16[1552,128]{1,0:T(8,128)(2,1)S(1)}, u32[]{:S(2)}, u32[]{:S(2)}) collective-permute-start(bf16[1552,128]{1,0:T(8,128)(2,1)} %get-tuple-element.46), channel_id=1, source_target_pairs={{0,8},{4,12},{8,0},{12,4},{16,24},{20,28},{24,16},{28,20},{1,9},{5... | collective-permute-start | bytes 1191944 | tf_op jit(solution)/shard_map/ppermute | solution.py:278
  10.2 1.4 collective-permute-start.9
  11.6 1.5 collective-permute-start.10
  13.2 9.7 %collective-permute-done.1.refs_2_.refs_10_ = bf16[512,128]{1,0:T(8,128)(2,1)S(1)} collective-permute-done((bf16[512,128]{1,0:T(8,128)(2,1)}, bf16[512,128]{1,0:T(8,128)(2,1)S(1)}, u32[]{:S(2)}, u32[]{:S(2)}) %collective-permute-start.1) | collective-permute-done | bytes 131104 | tf_op jit(solution)/shard_map/ppermute | solution.py:278
  22.8 0.8 collective-permute-start.11
  23.6 2.2 %collective-permute-start.12 = (bf16[1552,128]{1,0:T(8,128)(2,1)}, bf16[1552,128]{1,0:T(8,128)(2,1)S(1)}, u32[]{:S(2)}, u32[]{:S(2)}) collective-permute-start(bf16[1552,128]{1,0:T(8,128)(2,1)} %get-tuple-element.50), channel_id=1, source_target_pairs={{0,24},{4,28},{8,16},{12,20},{16,8},{20,12},{24,0},{28,4},{1,25},{... | collective-permute-start | bytes 1191944 | tf_op jit(solution)/shard_map/ppermute | solution.py:278
  25.8 1.4 collective-permute-start.13
  27.2 3.7 %collective-permute-done.9.refs_3_ = bf16[1552,128]{1,0:T(8,128)(2,1)S(1)} collective-permute-done((bf16[1552,128]{1,0:T(8,128)(2,1)}, bf16[1552,128]{1,0:T(8,128)(2,1)S(1)}, u32[]{:S(2)}, u32[]{:S(2)}) %collective-permute-start.9) | collective-permute-done | bytes 397344 | tf_op jit(solution)/shard_map/ppermute | solution.py:278
  30.9 2.1 %collective-permute-start.2 = (bf16[512,128]{1,0:T(8,128)(2,1)}, bf16[512,128]{1,0:T(8,128)(2,1)S(1)}, u32[]{:S(2)}, u32[]{:S(2)}) collective-permute-start(bf16[512,128]{1,0:T(8,128)(2,1)} %get-tuple-element.39), channel_id=1, source_target_pairs={{0,12},{4,8},{8,4},{12,0},{16,28},{20,24},{24,20},{28,16},{1,13},{... | collective-permute-start | bytes 393224 | tf_op jit(solution)/shard_map/ppermute | solution.py:278
  33.0 1.5 collective-permute-start.3
  34.6 16.6 %collective-permute-done.11.refs_5_ = bf16[1552,128]{1,0:T(8,128)(2,1)S(1)} collective-permute-done((bf16[1552,128]{1,0:T(8,128)(2,1)}, bf16[1552,128]{1,0:T(8,128)(2,1)S(1)}, u32[]{:S(2)}, u32[]{:S(2)}) %collective-permute-start.11) | collective-permute-done | bytes 397344 | tf_op jit(solution)/shard_map/ppermute | solution.py:278
  51.1 1.0 collective-permute-start.4
  52.1 2.5 %collective-permute-start.5 = (bf16[512,128]{1,0:T(8,128)(2,1)}, bf16[512,128]{1,0:T(8,128)(2,1)S(1)}, u32[]{:S(2)}, u32[]{:S(2)}) collective-permute-start(bf16[512,128]{1,0:T(8,128)(2,1)} %get-tuple-element.42), channel_id=1, source_target_pairs={{0,24},{4,28},{8,16},{12,20},{16,8},{20,12},{24,0},{28,4},{1,25},{... | collective-permute-start | bytes 393224 | tf_op jit(solution)/shard_map/ppermute | solution.py:278
  54.7 1.2 collective-permute-start.6
  55.9 20.1 %forward.1 = (bf16[8,4,512,512]{3,2,1,0:T(8,128)(2,1)}, f32[8,128,512]{2,1,0:T(8,128)}, bf16[8,512,128]{2,1,0:T(8,128)(2,1)}, f32[8,1,512]{2,1,0:T(1,128)}, f32[8,1,512]{2,1,0:T(1,128)}) custom-call(s32[1]{0:T(128)} %bitcast.rank_ref, bf16[1552,128]{1,0:T(8,128)(2,1)} %get-tuple-element.44.refs_0_, bf16[1552,128]{1,0:T(8,128)(2,1)} %copy-done, ...), custom_call_target="tpu_custom_call" | custom-call | tf_op jit(solution)/shard_map/forward/pallas_call | solution.py:315
  76.9 3.9 %project.1 = f32[2,4096]{1,0:T(2,128)} custom-call(s32[1]{0:T(128)} %bitcast.rank_ref, bf16[512,128]{1,0:T(8,128)(2,1)} %get-tuple-element.36.refs_0_.refs_8_, bf16[512,128]{1,0:T(8,128)(2,1)} %copy-done.7, bf16[512,128]{1,0:T(8,128)(2,1)} %copy-done.8, bf16[512,128]{1,0:T(8,128)(2,1)} %copy-done.9, bf16[512,128]{1,0:T(8,128)(2,1)} %copy-done.10, ...), custom_call_target="tpu_custom_call" | custom-call | tf_op jit(solution)/shard_map/project/pallas_call | solution.py:347
  81.0 1.4 collective-permute-done.14
  82.4 0.8 add.49
  83.1 1.5 collective-permute-start.17
  84.7 1.5 collective-permute-start.16
  86.7 1.3 collective-permute-done.17
  88.6 1.5 collective-permute-done.15
  90.1 3.7 %collective-permute-start.20 = (f32[2,4096]{1,0:T(2,128)S(1)}, f32[2,4096]{1,0:T(2,128)S(1)}, u32[]{:S(2)}, u32[]{:S(2)}) collective-permute-start(f32[2,4096]{1,0:T(2,128)S(1)} %add_add_fusion.1), channel_id=1, source_target_pairs={{0,3},{1,0},{2,1},{3,2},{4,7},{5,4},{6,5},{7,6},{8,11},{9,8},{10,9... | collective-permute-start | bytes 98312 | tf_op jit(solution)/shard_map/ppermute | solution.py:286
  93.8 1.0 collective-permute-start.18
  94.8 2.0 %dynamic-slice_bitcast_fusion = (bf16[512,128]{1,0:T(8,128)(2,1)S(1)}, bf16[512,128]{1,0:T(8,128)(2,1)S(1)}, bf16[512,128]{1,0:T(8,128)(2,1)S(1)}, bf16[512,128]...) fusion(bf16[8,512,128]{2,1,0:T(8,128)(2,1)} %get-tuple-element., ...), kind=kLoop, calls=%fused_computation | loop fusion | bytes 2097184 | tf_op jit(solution)/shard_map/jit(dynamic_index_in_dim)/squeeze | solution.py:362
  96.8 1.8 collective-permute-done.19
  98.6 0.9 collective-permute-done.18
  100.1 26.4 %backward.1 = (bf16[1536,128]{1,0:T(8,128)(2,1)}, bf16[1536,128]{1,0:T(8,128)(2,1)}, bf16[1536,128]{1,0:T(8,128)(2,1)}, bf16[1536,128]{1,0:T(8,128)(2,1)}, bf16[...) custom-call(s32[1]{0:T(128)} %bitcast.rank_ref, ...), custom_call_target="tpu_custom_call" | custom-call | tf_op jit(solution)/shard_map/backward/pallas_call | solution.py:375
  127.2 1.5 collective-permute-start.22
  128.7 0.7 collective-permute-start.24
  129.4 12.2 %collective-permute-done.22.refs_2_ = bf16[512,128]{1,0:T(8,128)(2,1)S(1)} collective-permute-done((bf16[512,128]{1,0:T(8,128)(2,1)S(1)}, bf16[512,128]{1,0:T(8,128)(2,1)S(1)}, u32[]{:S(2)}, u32[]{:S(2)}) %collective-permute-start.22) | collective-permute-done | bytes 131104 | tf_op jit(solution)/shard_map/ppermute | solution.py:278
  141.6 1.9 collective-permute-done.23.refs_3_
  143.5 0.7 collective-permute-start.26
  144.2 1.8 collective-permute-start.27
  146.0 0.8 collective-permute-done.25.refs_5_
  146.8 3.9 %collective-permute-done.26.refs_6_ = bf16[512,128]{1,0:T(8,128)(2,1)S(1)} collective-permute-done((bf16[512,128]{1,0:T(8,128)(2,1)S(1)}, bf16[512,128]{1,0:T(8,128)(2,1)S(1)}, u32[]{:S(2)}, u32[]{:S(2)}) %collective-permute-start.26) | collective-permute-done | bytes 131104 | tf_op jit(solution)/shard_map/ppermute | solution.py:278
  151.3 0.9 collective-permute-done.27.refs_7_
  152.2 1.3 collective-permute-start.32
  153.5 0.8 collective-permute-start.33
  154.4 1.6 collective-permute-start.34
  156.0 1.3 dynamic-slice_bitcast_fusion.8.stats_ref
  157.3 2.7 %normed.1 = bf16[512,1024]{1,0:T(8,128)(2,1)} custom-call(s32[1]{0:T(128)} %bitcast.rank_ref, f32[1,2,512]{2,1,0:T(2,128)} %dynamic-slice_bitcast_fusion.8.stats_ref, bf16[512,128]{1,0:T(8,128)(2,1)} %get-tuple-element.75.refs_0_, bf16[512,128]{1,0:T(8,128)(2,1)} %copy-done.21, bf16[512,128]{1,0:T(8,128)(2,1)} %copy-done.22, bf16[512,128]{1,0:T(8,128)(2,1)} %copy-done.23, ...), custom_call_target="tpu_custom_call" | custom-call | tf_op jit(solution)/shard_map/normed/pallas_call | solution.py:366
  160.1 19.7 %collective-permute-done.31.refs_4_ = bf16[1536,128]{1,0:T(8,128)(2,1)S(1)} collective-permute-done((bf16[1536,128]{1,0:T(8,128)(2,1)}, bf16[1536,128]{1,0:T(8,128)(2,1)S(1)}, u32[]{:S(2)}, u32[]{:S(2)}) %collective-permute-start.31) | collective-permute-done | bytes 393248 | tf_op jit(solution)/shard_map/ppermute | solution.py:278
  179.8 7.9 %collective-permute-done.32.refs_5_ = bf16[1536,128]{1,0:T(8,128)(2,1)S(1)} collective-permute-done((bf16[1536,128]{1,0:T(8,128)(2,1)}, bf16[1536,128]{1,0:T(8,128)(2,1)S(1)}, u32[]{:S(2)}, u32[]{:S(2)}) %collective-permute-start.32) | collective-permute-done | bytes 393248 | tf_op jit(solution)/shard_map/ppermute | solution.py:278
  187.7 0.7 copy-done.18
  188.7 3.8 %unpack.1 = (bf16[512,1024]{1,0:T(8,128)(2,1)}, bf16[512,1024]{1,0:T(8,128)(2,1)}, bf16[512,1024]{1,0:T(8,128)(2,1)}) custom-call(s32[1]{0:T(128)} %bitcast.rank_ref, bf16[1536,128]{1,0:T(8,128)(2,1)} %get-tuple-element.57.refs_0_, bf16[1536,128]{1,0:T(8,128)(2,1)} %copy-done.14, bf16[1536,128]{1,0:T(8,128)(2,1)} %copy-done.15, ...), custom_call_target="tpu_custom_call" | custom-call | tf_op jit(solution)/shard_map/unpack/pallas_call | solution.py:402
  (91 shorter events, 5.9 us)
Async XLA Ops:
  6.7 17.0 %collective-permute-start.7 = (bf16[1552,128]{1,0:T(8,128)(2,1)}, bf16[1552,128]{1,0:T(8,128)(2,1)S(1)}, u32[]{:S(2)}, u32[]{:S(2)}) collective-permute-start(bf16[1552,128]{1,0:T(8,128)(2,1)} %get-tuple-element.45), channel_id=1, source_target_pairs={{0,4},{4,0},{8,12},{12,8},{16,20},{20,16},{24,28},{28,24},{1,5},{5... | collective-permute-start | bytes 1191944 | tf_op jit(solution)/shard_map/ppermute | solution.py:278
  7.2 18.6 %collective-permute-start.8 = (bf16[1552,128]{1,0:T(8,128)(2,1)}, bf16[1552,128]{1,0:T(8,128)(2,1)S(1)}, u32[]{:S(2)}, u32[]{:S(2)}) collective-permute-start(bf16[1552,128]{1,0:T(8,128)(2,1)} %get-tuple-element.46), channel_id=1, source_target_pairs={{0,8},{4,12},{8,0},{12,4},{16,24},{20,28},{24,16},{28,20},{1,9},{5... | collective-permute-start | bytes 1191944 | tf_op jit(solution)/shard_map/ppermute | solution.py:278
  9.8 1.9 collective-permute-start
  9.9 12.9 %collective-permute-start.1 = (bf16[512,128]{1,0:T(8,128)(2,1)}, bf16[512,128]{1,0:T(8,128)(2,1)S(1)}, u32[]{:S(2)}, u32[]{:S(2)}) collective-permute-start(bf16[512,128]{1,0:T(8,128)(2,1)} %get-tuple-element.38), channel_id=1, source_target_pairs={{0,8},{4,12},{8,0},{12,4},{16,24},{20,28},{24,16},{28,20},{1,9},{5... | collective-permute-start | bytes 393224 | tf_op jit(solution)/shard_map/ppermute | solution.py:278
  10.2 20.7 %collective-permute-start.9 = (bf16[1552,128]{1,0:T(8,128)(2,1)}, bf16[1552,128]{1,0:T(8,128)(2,1)S(1)}, u32[]{:S(2)}, u32[]{:S(2)}) collective-permute-start(bf16[1552,128]{1,0:T(8,128)(2,1)} %get-tuple-element.47), channel_id=1, source_target_pairs={{0,12},{4,8},{8,4},{12,0},{16,28},{20,24},{24,20},{28,16},{1,13},{... | collective-permute-start | bytes 1191944 | tf_op jit(solution)/shard_map/ppermute | solution.py:278
  11.6 64.5 %copy-start.7 = (bf16[512,128]{1,0:T(8,128)(2,1)}, bf16[512,128]{1,0:T(8,128)(2,1)S(1)}, u32[]{:S(2)}) copy-start(bf16[512,128]{1,0:T(8,128)(2,1)S(1)} %collective-permute-done.refs_1_.refs_9_) | copy-start | bytes 393220
  11.6 21.4 %collective-permute-start.10 = (bf16[1552,128]{1,0:T(8,128)(2,1)}, bf16[1552,128]{1,0:T(8,128)(2,1)S(1)}, u32[]{:S(2)}, u32[]{:S(2)}) collective-permute-start(bf16[1552,128]{1,0:T(8,128)(2,1)} %get-tuple-element.48), channel_id=1, source_target_pairs={{0,16},{4,20},{8,24},{12,28},{16,0},{20,4},{24,8},{28,12},{1,17},{... | collective-permute-start | bytes 1191944 | tf_op jit(solution)/shard_map/ppermute | solution.py:278
  22.8 53.3 %copy-start.8 = (bf16[512,128]{1,0:T(8,128)(2,1)}, bf16[512,128]{1,0:T(8,128)(2,1)S(1)}, u32[]{:S(2)}) copy-start(bf16[512,128]{1,0:T(8,128)(2,1)S(1)} %collective-permute-done.1.refs_2_.refs_10_) | copy-start | bytes 393220
  22.8 28.3 %collective-permute-start.11 = (bf16[1552,128]{1,0:T(8,128)(2,1)}, bf16[1552,128]{1,0:T(8,128)(2,1)S(1)}, u32[]{:S(2)}, u32[]{:S(2)}) collective-permute-start(bf16[1552,128]{1,0:T(8,128)(2,1)} %get-tuple-element.49), channel_id=1, source_target_pairs={{0,20},{4,16},{8,28},{12,24},{16,4},{20,0},{24,12},{28,8},{1,21},{... | collective-permute-start | bytes 1191944 | tf_op jit(solution)/shard_map/ppermute | solution.py:278
  23.6 32.2 %copy-start = (bf16[1552,128]{1,0:T(8,128)(2,1)}, bf16[1552,128]{1,0:T(8,128)(2,1)S(1)}, u32[]{:S(2)}) copy-start(bf16[1552,128]{1,0:T(8,128)(2,1)S(1)} %collective-permute-done.7.refs_1_) | copy-start | bytes 1191940
  23.6 28.5 %collective-permute-start.12 = (bf16[1552,128]{1,0:T(8,128)(2,1)}, bf16[1552,128]{1,0:T(8,128)(2,1)S(1)}, u32[]{:S(2)}, u32[]{:S(2)}) collective-permute-start(bf16[1552,128]{1,0:T(8,128)(2,1)} %get-tuple-element.50), channel_id=1, source_target_pairs={{0,24},{4,28},{8,16},{12,20},{16,8},{20,12},{24,0},{28,4},{1,25},{... | collective-permute-start | bytes 1191944 | tf_op jit(solution)/shard_map/ppermute | solution.py:278
  25.8 30.1 %copy-start.1 = (bf16[1552,128]{1,0:T(8,128)(2,1)}, bf16[1552,128]{1,0:T(8,128)(2,1)S(1)}, u32[]{:S(2)}) copy-start(bf16[1552,128]{1,0:T(8,128)(2,1)S(1)} %collective-permute-done.8.refs_2_) | copy-start | bytes 1191940
  25.8 28.8 %collective-permute-start.13 = (bf16[1552,128]{1,0:T(8,128)(2,1)}, bf16[1552,128]{1,0:T(8,128)(2,1)S(1)}, u32[]{:S(2)}, u32[]{:S(2)}) collective-permute-start(bf16[1552,128]{1,0:T(8,128)(2,1)} %get-tuple-element.51), channel_id=1, source_target_pairs={{0,28},{4,24},{8,20},{12,16},{16,12},{20,8},{24,4},{28,0},{1,29},{... | collective-permute-start | bytes 1191944 | tf_op jit(solution)/shard_map/ppermute | solution.py:278
  30.9 25.0 %copy-start.2 = (bf16[1552,128]{1,0:T(8,128)(2,1)}, bf16[1552,128]{1,0:T(8,128)(2,1)S(1)}, u32[]{:S(2)}) copy-start(bf16[1552,128]{1,0:T(8,128)(2,1)S(1)} %collective-permute-done.9.refs_3_) | copy-start | bytes 1191940
  30.9 45.1 %collective-permute-start.2 = (bf16[512,128]{1,0:T(8,128)(2,1)}, bf16[512,128]{1,0:T(8,128)(2,1)S(1)}, u32[]{:S(2)}, u32[]{:S(2)}) collective-permute-start(bf16[512,128]{1,0:T(8,128)(2,1)} %get-tuple-element.39), channel_id=1, source_target_pairs={{0,12},{4,8},{8,4},{12,0},{16,28},{20,24},{24,20},{28,16},{1,13},{... | collective-permute-start | bytes 393224 | tf_op jit(solution)/shard_map/ppermute | solution.py:278
  33.0 22.9 %copy-start.3 = (bf16[1552,128]{1,0:T(8,128)(2,1)}, bf16[1552,128]{1,0:T(8,128)(2,1)S(1)}, u32[]{:S(2)}) copy-start(bf16[1552,128]{1,0:T(8,128)(2,1)S(1)} %collective-permute-done.10.refs_4_) | copy-start | bytes 1191940
  33.0 43.0 %collective-permute-start.3 = (bf16[512,128]{1,0:T(8,128)(2,1)}, bf16[512,128]{1,0:T(8,128)(2,1)S(1)}, u32[]{:S(2)}, u32[]{:S(2)}) collective-permute-start(bf16[512,128]{1,0:T(8,128)(2,1)} %get-tuple-element.40), channel_id=1, source_target_pairs={{0,16},{4,20},{8,24},{12,28},{16,0},{20,4},{24,8},{28,12},{1,17},{... | collective-permute-start | bytes 393224 | tf_op jit(solution)/shard_map/ppermute | solution.py:278
  51.1 25.0 %collective-permute-start.4 = (bf16[512,128]{1,0:T(8,128)(2,1)}, bf16[512,128]{1,0:T(8,128)(2,1)S(1)}, u32[]{:S(2)}, u32[]{:S(2)}) collective-permute-start(bf16[512,128]{1,0:T(8,128)(2,1)} %get-tuple-element.41), channel_id=1, source_target_pairs={{0,20},{4,16},{8,28},{12,24},{16,4},{20,0},{24,12},{28,8},{1,21},{... | collective-permute-start | bytes 393224 | tf_op jit(solution)/shard_map/ppermute | solution.py:278
  52.1 24.0 %collective-permute-start.5 = (bf16[512,128]{1,0:T(8,128)(2,1)}, bf16[512,128]{1,0:T(8,128)(2,1)S(1)}, u32[]{:S(2)}, u32[]{:S(2)}) collective-permute-start(bf16[512,128]{1,0:T(8,128)(2,1)} %get-tuple-element.42), channel_id=1, source_target_pairs={{0,24},{4,28},{8,16},{12,20},{16,8},{20,12},{24,0},{28,4},{1,25},{... | collective-permute-start | bytes 393224 | tf_op jit(solution)/shard_map/ppermute | solution.py:278
  54.7 21.5 %collective-permute-start.6 = (bf16[512,128]{1,0:T(8,128)(2,1)}, bf16[512,128]{1,0:T(8,128)(2,1)S(1)}, u32[]{:S(2)}, u32[]{:S(2)}) collective-permute-start(bf16[512,128]{1,0:T(8,128)(2,1)} %get-tuple-element.43), channel_id=1, source_target_pairs={{0,28},{4,24},{8,20},{12,16},{16,12},{20,8},{24,4},{28,0},{1,29},{... | collective-permute-start | bytes 393224 | tf_op jit(solution)/shard_map/ppermute | solution.py:278
  80.9 1.5 collective-permute-start.14
  83.1 4.9 %collective-permute-start.17 = (f32[2,4096]{1,0:T(2,128)S(1)}, f32[2,4096]{1,0:T(2,128)S(1)}, u32[]{:S(2)}, u32[]{:S(2)}) collective-permute-start(f32[2,4096]{1,0:T(2,128)S(1)} %add.49), channel_id=1, source_target_pairs={{0,24},{4,28},{8,16},{12,20},{16,8},{20,12},{24,0},{28,4},{1,25},{... | collective-permute-start | bytes 98312 | tf_op jit(solution)/shard_map/ppermute | solution.py:278
  84.7 3.9 %collective-permute-start.16 = (f32[2,4096]{1,0:T(2,128)S(1)}, f32[2,4096]{1,0:T(2,128)S(1)}, u32[]{:S(2)}, u32[]{:S(2)}) collective-permute-start(f32[2,4096]{1,0:T(2,128)S(1)} %add.49), channel_id=1, source_target_pairs={{0,16},{4,20},{8,24},{12,28},{16,0},{20,4},{24,8},{28,12},{1,17},{... | collective-permute-start | bytes 98312 | tf_op jit(solution)/shard_map/ppermute | solution.py:278
  86.2 3.9 %collective-permute-start.15 = (f32[2,4096]{1,0:T(2,128)S(1)}, f32[2,4096]{1,0:T(2,128)S(1)}, u32[]{:S(2)}, u32[]{:S(2)}) collective-permute-start(f32[2,4096]{1,0:T(2,128)S(1)} %add.49), channel_id=1, source_target_pairs={{0,8},{4,12},{8,0},{12,4},{16,24},{20,28},{24,16},{28,20},{1,9},{5... | collective-permute-start | bytes 98312 | tf_op jit(solution)/shard_map/ppermute | solution.py:278
  90.1 6.7 %collective-permute-start.20 = (f32[2,4096]{1,0:T(2,128)S(1)}, f32[2,4096]{1,0:T(2,128)S(1)}, u32[]{:S(2)}, u32[]{:S(2)}) collective-permute-start(f32[2,4096]{1,0:T(2,128)S(1)} %add_add_fusion.1), channel_id=1, source_target_pairs={{0,3},{1,0},{2,1},{3,2},{4,7},{5,4},{6,5},{7,6},{8,11},{9,8},{10,9... | collective-permute-start | bytes 98312 | tf_op jit(solution)/shard_map/ppermute | solution.py:286
  93.8 4.8 %collective-permute-start.19 = (f32[2,4096]{1,0:T(2,128)S(1)}, f32[2,4096]{1,0:T(2,128)S(1)}, u32[]{:S(2)}, u32[]{:S(2)}) collective-permute-start(f32[2,4096]{1,0:T(2,128)S(1)} %add_add_fusion.1), channel_id=1, source_target_pairs={{0,2},{1,3},{2,0},{3,1},{4,6},{5,7},{6,4},{7,5},{8,10},{9,11},{10,... | collective-permute-start | bytes 98312 | tf_op jit(solution)/shard_map/ppermute | solution.py:286
  93.8 5.7 %collective-permute-start.18 = (f32[2,4096]{1,0:T(2,128)S(1)}, f32[2,4096]{1,0:T(2,128)S(1)}, u32[]{:S(2)}, u32[]{:S(2)}) collective-permute-start(f32[2,4096]{1,0:T(2,128)S(1)} %add_add_fusion.1), channel_id=1, source_target_pairs={{0,1},{1,2},{2,3},{3,0},{4,5},{5,6},{6,7},{7,4},{8,9},{9,10},{10,1... | collective-permute-start | bytes 98312 | tf_op jit(solution)/shard_map/ppermute | solution.py:286
  96.8 31.9 %collective-permute-start.21 = (bf16[512,128]{1,0:T(8,128)(2,1)S(1)}, bf16[512,128]{1,0:T(8,128)(2,1)S(1)}, u32[]{:S(2)}, u32[]{:S(2)}) collective-permute-start(bf16[512,128]{1,0:T(8,128)(2,1)S(1)} %get-tuple-element.74), channel_id=1, source_target_pairs={{0,4},{4,0},{8,12},{12,8},{16,20},{20,16},{24,28},{28,24},{1,5},{5... | collective-permute-start | bytes 393224 | tf_op jit(solution)/shard_map/ppermute | solution.py:278
  126.5 27.0 %collective-permute-start.28 = (bf16[1536,128]{1,0:T(8,128)(2,1)}, bf16[1536,128]{1,0:T(8,128)(2,1)S(1)}, u32[]{:S(2)}, u32[]{:S(2)}) collective-permute-start(bf16[1536,128]{1,0:T(8,128)(2,1)} %get-tuple-element.58), channel_id=1, source_target_pairs={{0,4},{4,0},{8,12},{12,8},{16,20},{20,16},{24,28},{28,24},{1,5},{5... | collective-permute-start | bytes 1179656 | tf_op jit(solution)/shard_map/ppermute | solution.py:278
  126.6 27.8 %collective-permute-start.29 = (bf16[1536,128]{1,0:T(8,128)(2,1)}, bf16[1536,128]{1,0:T(8,128)(2,1)S(1)}, u32[]{:S(2)}, u32[]{:S(2)}) collective-permute-start(bf16[1536,128]{1,0:T(8,128)(2,1)} %get-tuple-element.59), channel_id=1, source_target_pairs={{0,8},{4,12},{8,0},{12,4},{16,24},{20,28},{24,16},{28,20},{1,9},{5... | collective-permute-start | bytes 1179656 | tf_op jit(solution)/shard_map/ppermute | solution.py:278
  127.2 14.4 %collective-permute-start.22 = (bf16[512,128]{1,0:T(8,128)(2,1)S(1)}, bf16[512,128]{1,0:T(8,128)(2,1)S(1)}, u32[]{:S(2)}, u32[]{:S(2)}) collective-permute-start(bf16[512,128]{1,0:T(8,128)(2,1)S(1)} %get-tuple-element.73), channel_id=1, source_target_pairs={{0,8},{4,12},{8,0},{12,4},{16,24},{20,28},{24,16},{28,20},{1,9},{5... | collective-permute-start | bytes 393224 | tf_op jit(solution)/shard_map/ppermute | solution.py:278
  128.7 14.8 %collective-permute-start.23 = (bf16[512,128]{1,0:T(8,128)(2,1)S(1)}, bf16[512,128]{1,0:T(8,128)(2,1)S(1)}, u32[]{:S(2)}, u32[]{:S(2)}) collective-permute-start(bf16[512,128]{1,0:T(8,128)(2,1)S(1)} %get-tuple-element.72), channel_id=1, source_target_pairs={{0,12},{4,8},{8,4},{12,0},{16,28},{20,24},{24,20},{28,16},{1,13},{... | collective-permute-start | bytes 393224 | tf_op jit(solution)/shard_map/ppermute | solution.py:278
  128.7 28.5 %copy-start.21 = (bf16[512,128]{1,0:T(8,128)(2,1)}, bf16[512,128]{1,0:T(8,128)(2,1)S(1)}, u32[]{:S(2)}) copy-start(bf16[512,128]{1,0:T(8,128)(2,1)S(1)} %collective-permute-done.21.refs_1_) | copy-start | bytes 393220
  128.7 15.5 %collective-permute-start.24 = (bf16[512,128]{1,0:T(8,128)(2,1)S(1)}, bf16[512,128]{1,0:T(8,128)(2,1)S(1)}, u32[]{:S(2)}, u32[]{:S(2)}) collective-permute-start(bf16[512,128]{1,0:T(8,128)(2,1)S(1)} %get-tuple-element.71), channel_id=1, source_target_pairs={{0,16},{4,20},{8,24},{12,28},{16,0},{20,4},{24,8},{28,12},{1,17},{... | collective-permute-start | bytes 393224 | tf_op jit(solution)/shard_map/ppermute | solution.py:278
  141.6 15.7 %copy-start.22 = (bf16[512,128]{1,0:T(8,128)(2,1)}, bf16[512,128]{1,0:T(8,128)(2,1)S(1)}, u32[]{:S(2)}) copy-start(bf16[512,128]{1,0:T(8,128)(2,1)S(1)} %collective-permute-done.22.refs_2_) | copy-start | bytes 393220
  141.6 5.2 %collective-permute-start.25 = (bf16[512,128]{1,0:T(8,128)(2,1)S(1)}, bf16[512,128]{1,0:T(8,128)(2,1)S(1)}, u32[]{:S(2)}, u32[]{:S(2)}) collective-permute-start(bf16[512,128]{1,0:T(8,128)(2,1)S(1)} %get-tuple-element.70), channel_id=1, source_target_pairs={{0,20},{4,16},{8,28},{12,24},{16,4},{20,0},{24,12},{28,8},{1,21},{... | collective-permute-start | bytes 393224 | tf_op jit(solution)/shard_map/ppermute | solution.py:278
  143.5 13.8 %copy-start.23 = (bf16[512,128]{1,0:T(8,128)(2,1)}, bf16[512,128]{1,0:T(8,128)(2,1)S(1)}, u32[]{:S(2)}) copy-start(bf16[512,128]{1,0:T(8,128)(2,1)S(1)} %collective-permute-done.23.refs_3_) | copy-start | bytes 393220
  143.5 7.2 %collective-permute-start.26 = (bf16[512,128]{1,0:T(8,128)(2,1)S(1)}, bf16[512,128]{1,0:T(8,128)(2,1)S(1)}, u32[]{:S(2)}, u32[]{:S(2)}) collective-permute-start(bf16[512,128]{1,0:T(8,128)(2,1)S(1)} %get-tuple-element.69), channel_id=1, source_target_pairs={{0,24},{4,28},{8,16},{12,20},{16,8},{20,12},{24,0},{28,4},{1,25},{... | collective-permute-start | bytes 393224 | tf_op jit(solution)/shard_map/ppermute | solution.py:278
  144.2 13.1 %copy-start.24 = (bf16[512,128]{1,0:T(8,128)(2,1)}, bf16[512,128]{1,0:T(8,128)(2,1)S(1)}, u32[]{:S(2)}) copy-start(bf16[512,128]{1,0:T(8,128)(2,1)S(1)} %collective-permute-done.24.refs_4_) | copy-start | bytes 393220
  144.2 8.0 %collective-permute-start.27 = (bf16[512,128]{1,0:T(8,128)(2,1)S(1)}, bf16[512,128]{1,0:T(8,128)(2,1)S(1)}, u32[]{:S(2)}, u32[]{:S(2)}) collective-permute-start(bf16[512,128]{1,0:T(8,128)(2,1)S(1)} %get-tuple-element.68), channel_id=1, source_target_pairs={{0,28},{4,24},{8,20},{12,16},{16,12},{20,8},{24,4},{28,0},{1,29},{... | collective-permute-start | bytes 393224 | tf_op jit(solution)/shard_map/ppermute | solution.py:278
  146.8 13.3 %collective-permute-start.30 = (bf16[1536,128]{1,0:T(8,128)(2,1)}, bf16[1536,128]{1,0:T(8,128)(2,1)S(1)}, u32[]{:S(2)}, u32[]{:S(2)}) collective-permute-start(bf16[1536,128]{1,0:T(8,128)(2,1)} %get-tuple-element.60), channel_id=1, source_target_pairs={{0,12},{4,8},{8,4},{12,0},{16,28},{20,24},{24,20},{28,16},{1,13},{... | collective-permute-start | bytes 1179656 | tf_op jit(solution)/shard_map/ppermute | solution.py:278
  150.7 29.0 %collective-permute-start.31 = (bf16[1536,128]{1,0:T(8,128)(2,1)}, bf16[1536,128]{1,0:T(8,128)(2,1)S(1)}, u32[]{:S(2)}, u32[]{:S(2)}) collective-permute-start(bf16[1536,128]{1,0:T(8,128)(2,1)} %get-tuple-element.61), channel_id=1, source_target_pairs={{0,16},{4,20},{8,24},{12,28},{16,0},{20,4},{24,8},{28,12},{1,17},{... | collective-permute-start | bytes 1179656 | tf_op jit(solution)/shard_map/ppermute | solution.py:278
  152.2 35.4 %collective-permute-start.32 = (bf16[1536,128]{1,0:T(8,128)(2,1)}, bf16[1536,128]{1,0:T(8,128)(2,1)S(1)}, u32[]{:S(2)}, u32[]{:S(2)}) collective-permute-start(bf16[1536,128]{1,0:T(8,128)(2,1)} %get-tuple-element.62), channel_id=1, source_target_pairs={{0,20},{4,16},{8,28},{12,24},{16,4},{20,0},{24,12},{28,8},{1,21},{... | collective-permute-start | bytes 1179656 | tf_op jit(solution)/shard_map/ppermute | solution.py:278
  153.5 34.1 %copy-start.14 = (bf16[1536,128]{1,0:T(8,128)(2,1)}, bf16[1536,128]{1,0:T(8,128)(2,1)S(1)}, u32[]{:S(2)}) copy-start(bf16[1536,128]{1,0:T(8,128)(2,1)S(1)} %collective-permute-done.28.refs_1_) | copy-start | bytes 1179652
  153.5 34.1 %collective-permute-start.33 = (bf16[1536,128]{1,0:T(8,128)(2,1)}, bf16[1536,128]{1,0:T(8,128)(2,1)S(1)}, u32[]{:S(2)}, u32[]{:S(2)}) collective-permute-start(bf16[1536,128]{1,0:T(8,128)(2,1)} %get-tuple-element.63), channel_id=1, source_target_pairs={{0,24},{4,28},{8,16},{12,20},{16,8},{20,12},{24,0},{28,4},{1,25},{... | collective-permute-start | bytes 1179656 | tf_op jit(solution)/shard_map/ppermute | solution.py:278
  154.4 33.3 %copy-start.15 = (bf16[1536,128]{1,0:T(8,128)(2,1)}, bf16[1536,128]{1,0:T(8,128)(2,1)S(1)}, u32[]{:S(2)}) copy-start(bf16[1536,128]{1,0:T(8,128)(2,1)S(1)} %collective-permute-done.29.refs_2_) | copy-start | bytes 1179652
  154.4 33.3 %collective-permute-start.34 = (bf16[1536,128]{1,0:T(8,128)(2,1)}, bf16[1536,128]{1,0:T(8,128)(2,1)S(1)}, u32[]{:S(2)}, u32[]{:S(2)}) collective-permute-start(bf16[1536,128]{1,0:T(8,128)(2,1)} %get-tuple-element.64), channel_id=1, source_target_pairs={{0,28},{4,24},{8,20},{12,16},{16,12},{20,8},{24,4},{28,0},{1,29},{... | collective-permute-start | bytes 1179656 | tf_op jit(solution)/shard_map/ppermute | solution.py:278
  160.0 27.6 %copy-start.16 = (bf16[1536,128]{1,0:T(8,128)(2,1)}, bf16[1536,128]{1,0:T(8,128)(2,1)S(1)}, u32[]{:S(2)}) copy-start(bf16[1536,128]{1,0:T(8,128)(2,1)S(1)} %collective-permute-done.30.refs_3_) | copy-start | bytes 1179652
  (15 other events, 46.3 us)
